TPU v7x, 32 devices: a whole 2x2x4 slice. The times are simulated.
32 devices in a mesh: dp: 16 (over z, y, x), mp: 2 (over core).
Axes of the slice: x: 2, y: 2, z: 4, core: 2. Of those that a mesh axis runs over, the one named last changes fastest.
Arguments:
- images: bfloat16 [32768, 384], P('dp'), may hold values from -6 to 6
- means: float32 [8192, 384], P(('mp', 'dp')), may hold values from -0.6 to 0.6
- precisions: float32 [8192, 384], P(('mp', 'dp')), may hold values from 0.5 to 2
- logits: float32 [8192], replicated, may hold values from -6 to 6
Outputs:
- new_means: float32 [8192, 384], P(('mp', 'dp'))
- new_variances: float32 [8192, 384], P(('mp', 'dp'))
- new_log_weights: float32 [8192], P(('mp', 'dp'))
- log_likelihood: float32 [32768], P('dp')
All inputs are finite; a program needn't handle non-finite values.
Results may differ from a plain program's by a relative error of at most 0.0039.
The roundings to bfloat16 on the way count: a program that leaves them out, or rounds other values in their place, can miss the bound.
Values may be sent and summed in bfloat16 or wider, within the bound.
A program may use at most 128 MiB of HBM per device.

v0:
```python
import math

import jax
import jax.numpy as jnp
from jax import lax
from jax.sharding import PartitionSpec as P

D = 384


def matmul_t(left, right):
    return lax.dot_general(
        left, right, (((1,), (1,)), ((), ())), preferred_element_type=jnp.float32
    )


def derive(means, precisions, logits):
    prec_b = precisions.astype(jnp.bfloat16)
    scaled = (means * precisions).astype(jnp.bfloat16)
    offset = (
        logits
        + 0.5 * jnp.sum(jnp.log(precisions) - means * means * precisions, axis=1)
        - 0.5 * D * math.log(2.0 * math.pi)
    )
    return (prec_b, scaled, offset)


def body(images, means, precisions, logits):
    squares = (images.astype(jnp.float32) * images.astype(jnp.float32)).astype(jnp.bfloat16)
    own_rows = means.shape[0]
    group_rows = own_rows * lax.axis_size("dp")
    own_start = lax.axis_index("mp") * group_rows + lax.axis_index("dp") * own_rows
    own_logits = lax.dynamic_slice_in_dim(logits, own_start, own_rows)
    own_prec, own_scaled, own_offset = derive(means, precisions, own_logits)
    prec_b, scaled = (
        lax.all_gather(own_prec, "dp", axis=0, tiled=True),
        lax.all_gather(own_scaled, "dp", axis=0, tiled=True),
    )
    offset = lax.all_gather(own_offset, "dp", axis=0, tiled=True)
    scores = -0.5 * matmul_t(squares, prec_b) + matmul_t(images, scaled) + offset[None, :]
    row_peak = jnp.max(scores, axis=1)
    logit_peak = jnp.max(logits)
    logit_total = logit_peak + jnp.log(jnp.sum(jnp.exp(logits - logit_peak)))
    row_high = lax.pmax(row_peak, "mp")
    local_rows = jnp.sum(jnp.exp(scores - row_high[:, None]), axis=1)
    row_sum = lax.psum(local_rows, "mp")
    row_total = row_high + jnp.log(row_sum)
    log_likelihood = row_total - logit_total
    shares = jnp.exp(scores - row_total[:, None]).astype(jnp.bfloat16)
    features = jnp.concatenate([images, squares], axis=1)
    counts = jnp.sum(shares.astype(jnp.float32), axis=0)
    moments = lax.dot_general(
        shares, features, (((0,), (0,)), ((), ())), preferred_element_type=jnp.float32
    )
    own_counts, own_moments = (
        lax.psum_scatter(counts, "dp", scatter_dimension=0, tiled=True),
        lax.psum_scatter(moments, "dp", scatter_dimension=0, tiled=True),
    )
    width = images.shape[1]
    total_images = images.shape[0] * lax.axis_size("dp")
    total_components = logits.shape[0]
    denominator = own_counts + 1.0
    new_means = (own_moments[:, :width] + means) / denominator[:, None]
    second = (own_moments[:, width:] + 1.0 / precisions + means * means) / denominator[:, None]
    new_variances = second - new_means * new_means
    new_log_weights = jnp.log(denominator) - jnp.log(jnp.float32(total_images + total_components))
    return (new_means, new_variances, new_log_weights, log_likelihood)


def solution(mesh):
    return jax.shard_map(
        body,
        mesh=mesh,
        in_specs=(P("dp", None), P(("mp", "dp"), None), P(("mp", "dp"), None), P()),
        out_specs=(P(("mp", "dp"), None), P(("mp", "dp"), None), P(("mp", "dp")), P("dp")),
        check_vma=False,
    )
```

profile of v0, /device:TPU:0, one launch (start us, length us, event | category | flops | bytes accessed | tf_op | source)
XLA Modules:
  0.0 428.7 jit_solution(15741560985601273215)
XLA Ops:
  7.2 2.1 subtract_reduce_fusion
  9.3 0.0 all-gather.6.cloned.1.call-start
  9.4 0.7 all-gather.6.cloned.1.call-update
  10.1 1.4 reduce_max.19
  11.5 2.0 exponential_reduce_fusion.1
  14.8 0.8 add_add_fusion
  15.6 42.6 %all-gather = f32[16,1,256]{2,1,0:T(1,128)S(1)} all-gather(f32[1,1,256]{2,1,0:T(1,128)S(1)} %bitcast.11), channel_id=1, replica_groups=mesh['dp'=16,'mp'=2] {'dp'}, dimensions={0}, use_global_device_ids=true | all-gather | bytes 17408 | tf_op jit(solution)/shard_map/all_gather | solution.py:39
  58.3 1.8 multiply_convert_fusion
  60.1 21.8 %all-gather.4.cloned.1.call-done = bf16[4096,384]{1,0:T(8,128)(2,1)} async-done(((bf16[256,384]{1,0:T(8,128)(2,1)}), bf16[4096,384]{1,0:T(8,128)(2,1)}) %all-gather.4.cloned.1.call-update) | async-done | bytes 3145744 | tf_op jit(solution)/shard_map/all_gather | solution.py:36
  81.9 17.3 %fusion.10 = f32[2048,4096]{1,0:T(8,128)} fusion(bf16[4096,384]{1,0:T(8,128)(2,1)} %all-gather.4.cloned.1.call-done, bf16[2048,384]{1,0:T(8,128)(2,1)} %param.4), kind=kOutput, calls=%fused_computation.25 | convolution fusion | flops 6444810240 | bytes 38273024 | tf_op jit(solution)/shard_map/dot_general | solution.py:12
  99.2 52.5 %all-gather.6.cloned.1.call-done = bf16[4096,384]{1,0:T(8,128)(2,1)} async-done(((bf16[256,384]{1,0:T(8,128)(2,1)}), bf16[4096,384]{1,0:T(8,128)(2,1)}) %all-gather.6.cloned.1.call-update) | async-done | bytes 3145744 | tf_op jit(solution)/shard_map/all_gather | solution.py:37
  151.7 24.4 %fusion.12 = (f32[2048]{0:T(1024)S(1)}, f32[2048,4096]{1,0:T(8,128)}) fusion(f32[4096]{0:T(1024)S(1)} %bitcast.10, bf16[4096,384]{1,0:T(8,128)(2,1)} %all-gather.6.cloned.1.call-done, bf16[2048,384]{1,0:T(8,128)(2,1)S(1)} %copy-done, f32[2048,4096]{1,0:T(8,128)} %fusion.10), kind=kOutput, calls=%fused_computation.26 | convolution fusion | flops 6476003328 | bytes 71852032 | tf_op jit(solution)/shard_map/dot_general | solution.py:12
  176.1 2.5 pmax.7
  178.5 13.6 %exponential_reduce_fusion = f32[2048]{0:T(1024)S(1)} fusion(f32[2048,4096]{1,0:T(8,128)} %get-tuple-element.14, f32[2048]{0:T(1024)S(1)} %pmax.7), kind=kLoop, calls=%fused_computation.4 | loop fusion | flops 16775168 | bytes 33570816 | tf_op jit(solution)/shard_map/reduce_sum | solution.py:45
  192.1 2.5 psum.7
  194.6 0.6 broadcast_subtract_fusion
  195.2 21.8 %fusion.1 = f32[4096,768]{1,0:T(8,128)} fusion(bf16[2048,384]{1,0:T(8,128)(2,1)S(1)} %multiply_convert_fusion, bf16[2048,384]{1,0:T(8,128)(2,1)S(1)} %copy-done, f32[2048,4096]{1,0:T(8,128)} %get-tuple-element.14, f32[2048]{0:T(1024)S(1)} %get-tuple-element.5), kind=kOutput, calls=%fused_computation.5 | convolution fusion | flops 12907970560 | bytes 49291264 | tf_op jit(solution)/shard_map/dot_general | solution.py:52
  217.1 0.6 copy-done.3
  217.7 0.6 dynamic-slice
  219.0 14.3 %convert_reduce_fusion = f32[4096]{0:T(1024)S(1)} fusion(f32[2048,4096]{1,0:T(8,128)} %get-tuple-element.14, f32[2048]{0:T(1024)S(1)} %get-tuple-element.5), kind=kLoop, calls=%fused_computation.2 | loop fusion | flops 33550336 | bytes 33579008 | tf_op jit(solution)/shard_map/reduce_sum | solution.py:51
  233.3 76.9 %all-reduce = f32[4096]{0:T(1024)S(1)} all-reduce(f32[4096]{0:T(1024)S(1)} %convert_reduce_fusion), channel_id=3, replica_groups=mesh['dp'=16,'mp'=2] {'dp'}, use_global_device_ids=true, to_apply=%region_7.0.clone | all-reduce | flops 4096 | bytes 32768
  310.2 0.6 log_add_fusion.1
  310.8 109.2 %reduce-scatter.2.cloned.1.call-done = f32[256,768]{1,0:T(8,128)} async-done(((f32[4096,768]{1,0:T(8,128)}), f32[256,768]{1,0:T(8,128)}) %reduce-scatter.2.cloned.1.call-update) | async-done | bytes 786448 | tf_op jit(solution)/shard_map/reduce_scatter | solution.py:57
  420.0 2.1 fusion.7
  (11 shorter events, 0.1 us)
Async XLA Ops:
  7.2 74.7 %all-gather.4.cloned.1.call-start = ((), (), s32[]{:S(2)}) async-start(), calls=%async_computation.1 | async-start | bytes 3342336 | tf_op jit(solution)/shard_map/all_gather | solution.py:36
  9.3 142.4 %all-gather.6.cloned.1.call-start = ((), (), s32[]{:S(2)}) async-start(), calls=%async_computation.2 | async-start | bytes 3342336 | tf_op jit(solution)/shard_map/all_gather | solution.py:37
  10.1 410.0 %reduce-scatter.2.cloned.1.call-start = ((), (), s32[]{:S(2)}) async-start(), calls=%async_computation.3 | async-start | bytes 13369344 | tf_op jit(solution)/shard_map/reduce_scatter | solution.py:57
  60.1 91.6 %copy-start = (bf16[2048,384]{1,0:T(8,128)(2,1)S(1)}, bf16[2048,384]{1,0:T(8,128)(2,1)}, u32[]{:S(2)}) copy-start(bf16[2048,384]{1,0:T(8,128)(2,1)} %param.4) | copy-start | bytes 4718596
  217.1 0.7 copy-start.3
  218.9 201.1 %copy-start.1 = (f32[256,384]{1,0:T(8,128)S(1)}, f32[256,384]{1,0:T(8,128)}, u32[]{:S(2)}) copy-start(f32[256,384]{1,0:T(8,128)} %param.6) | copy-start | bytes 1179652
  219.0 201.1 %copy-start.2 = (f32[256,384]{1,0:T(8,128)S(1)}, f32[256,384]{1,0:T(8,128)}, u32[]{:S(2)}) copy-start(f32[256,384]{1,0:T(8,128)} %param.5) | copy-start | bytes 1179652
Sparse Core Ops, SparseCore 0:
  11.3 70.5 all-gather.3
  85.2 66.3 all-gather.5
  217.2 202.7 reduce-scatter.1
where the time goes:
time: 429 us
  waiting for transfers between devices  184 us (43%)
  blocking collectives  125 us (29%)
  matrix products  63.5 us (15%)
  other arithmetic  39.4 us (9%)
  between operations  15.8 us (4%)
    reduce_scatter x1, waiting for transfers between devices, body(): lax.psum_scatter(moments, 'dp', scatter_dimension=0, tiled=True)  109 us
    unnamed x1, blocking collectives  76.9 us
    all_gather x1, waiting for transfers between devices, body(): lax.all_gather(own_scaled, 'dp', axis=0, tiled=True)  52.5 us
    all_gather x1, blocking collectives, body(): offset = lax.all_gather(own_offset, 'dp', axis=0, tiled=True)  42.6 us
    dot_general x2, matrix products, matmul_t(): lax.dot_general(left, right, (((1,), (1,)), ((), ())), preferred_element_...  41.7 us
    dot_general x1, matrix products, body(): lax.dot_general(shares, features, (((0,), (0,)), ((), ())), preferred_ele...  21.8 us
    all_gather x1, waiting for transfers between devices, body(): lax.all_gather(own_prec, 'dp', axis=0, tiled=True)  21.8 us
    reduce_sum x1, other arithmetic, body(): counts = jnp.sum(shares.astype(jnp.float32), axis=0)  14.3 us
  transfers between devices with their start and end apart: 3, of which 3 were waited for; matrix products, arithmetic and copies ran while one was open for 9% of the time, Pallas kernels for 0%

commit v1 on v0

v1 whole, which is shorter than its diff:
```python
import functools
import math

import jax
import jax.numpy as jnp
from jax import lax
from jax.experimental import pallas as pl
from jax.experimental.pallas import tpu as pltpu
from jax.sharding import Mesh, PartitionSpec as P

MESH = pl.DeviceIdType.MESH
SQUARE = 4
CHUNK = 512
F32 = jnp.float32
BF16 = jnp.bfloat16
VMEM_LIMIT = 60 * 1024 * 1024


def remote(src, dst, send, recv, device):
    return pltpu.make_async_remote_copy(
        src_ref=src, dst_ref=dst, send_sem=send, recv_sem=recv, device_id=device, device_id_type=MESH
    )


def gather_kernel(n_ca, img_ref, w_ref, off_ref, imgs_ref, wall_ref, offall_ref, stage,
                  loc, isend, irecv, wsend, wrecv, osend, orecv):
    a, b, m = lax.axis_index("ca"), lax.axis_index("ib"), lax.axis_index("mp")
    core = lax.rem(m, 2)
    partner = m + 1 - 2 * core
    bx = b + 1 - 2 * lax.rem(b, 2)
    by = lax.rem(b + 2, 4)
    bd = lax.rem(bx + 2, 4)
    to_x, to_y, to_p = (a, bx, m), (a, by, m), (a, b, partner)
    half_rows = img_ref.shape[0] // 2
    half = pl.ds(pl.multiple_of(core * half_rows, half_rows), half_rows)

    barrier = pltpu.get_barrier_semaphore()
    for dev in (to_x, to_y, to_p):
        pl.semaphore_signal(barrier, inc=1, device_id=dev, device_id_type=MESH)

    @pl.when(a > 0)
    def _():
        pl.semaphore_signal(barrier, inc=1, device_id=(a - 1, b, m), device_id_type=MESH)

    @pl.when(a < n_ca - 1)
    def _():
        pl.semaphore_signal(barrier, inc=1, device_id=(a + 1, b, m), device_id_type=MESH)

    own_in = pltpu.make_async_copy(img_ref, stage, loc.at[0])
    own_in.start()
    own_w = pltpu.make_async_copy(w_ref, wall_ref.at[a], loc.at[1])
    own_w.start()
    own_o = pltpu.make_async_copy(off_ref, offall_ref.at[a], loc.at[2])
    own_o.start()

    ends = (a == 0).astype(jnp.int32) + (a == n_ca - 1).astype(jnp.int32)
    pl.semaphore_wait(barrier, 5 - ends)

    def shard(i, src_own=False):
        src = img_ref.at[half] if src_own else imgs_ref.at[i, half]
        return src, imgs_ref.at[i, half]

    def img_copy(k, i, dev, src_own=False):
        src, dst = shard(i, src_own)
        return remote(src, dst, isend.at[k], irecv.at[k], dev)

    send_x = img_copy(0, b, to_x, True)
    send_y = img_copy(1, b, to_y, True)
    send_x.start()
    send_y.start()

    def chain(direction, s):
        blk = a - s if direction == 0 else a + s
        blk_ok = (blk >= 0) if direction == 0 else (blk < n_ca)
        nbr_ok = (a < n_ca - 1) if direction == 0 else (a > 0)
        nbr = a + 1 if direction == 0 else a - 1
        blk_c = jnp.clip(blk, 0, n_ca - 1)
        src_w = w_ref if s == 0 else wall_ref.at[blk_c]
        src_o = off_ref if s == 0 else offall_ref.at[blk_c]
        dev = (nbr, b, m)
        cw = remote(src_w, wall_ref.at[blk_c], wsend.at[direction, s], wrecv.at[direction, s], dev)
        co = remote(src_o, offall_ref.at[blk_c], osend.at[direction, s], orecv.at[direction, s], dev)
        return jnp.logical_and(blk_ok, nbr_ok), cw, co

    def chain_recv(direction, s):
        blk = a - 1 - s if direction == 0 else a + 1 + s
        ok = (blk >= 0) if direction == 0 else (blk < n_ca)
        blk_c = jnp.clip(blk, 0, n_ca - 1)
        nbr = jnp.clip(a + 1 if direction == 0 else a - 1, 0, n_ca - 1)
        dev = (nbr, b, m)
        cw = remote(w_ref, wall_ref.at[blk_c], wsend.at[direction, s], wrecv.at[direction, s], dev)
        co = remote(off_ref, offall_ref.at[blk_c], osend.at[direction, s], orecv.at[direction, s], dev)
        return ok, cw, co

    def start_chain(s):
        for d in (0, 1):
            ok, cw, co = chain(d, s)

            @pl.when(ok)
            def _():
                cw.start()
                co.start()

    def wait_chain(s):
        for d in (0, 1):
            ok, cw, co = chain_recv(d, s)

            @pl.when(ok)
            def _():
                cw.wait_recv()
                co.wait_recv()

    start_chain(0)
    own_in.wait()
    own_out = pltpu.make_async_copy(stage, imgs_ref.at[b], loc.at[0])
    own_out.start()
    wait_chain(0)
    if n_ca > 2:
        start_chain(1)
    send_x.wait_recv()
    pass_x = img_copy(3, bx, to_p)
    pass_x.start()

    @pl.when(core == 0)
    def _():
        img_copy(2, bx, to_y).start()

    send_y.wait_recv()
    pass_y = img_copy(4, by, to_p)
    pass_y.start()

    @pl.when(core == 1)
    def _():
        img_copy(2, by, to_x).start()

    for s in range(1, n_ca - 1):
        wait_chain(s)
        if s + 1 < n_ca - 1:
            start_chain(s + 1)
    relay = img_copy(2, bd, to_x)
    relay.wait_recv()
    pass_d = img_copy(5, bd, to_p)
    pass_d.start()
    for c in (pass_x, pass_y, pass_d):
        c.wait()
    for c in (send_x, send_y, relay):
        c.wait_send()
    for s in range(n_ca - 1):
        for d in (0, 1):
            ok, cw, co = chain(d, s)

            @pl.when(ok)
            def _():
                cw.wait_send()
                co.wait_send()
    own_out.wait()
    own_w.wait()
    own_o.wait()


def gather(images, w, off, n_ca):
    t, d = images.shape
    any_spec = pl.BlockSpec(memory_space=pl.ANY)
    vmem = pl.BlockSpec(memory_space=pltpu.VMEM)
    dma = pltpu.SemaphoreType.DMA
    return pl.pallas_call(
        functools.partial(gather_kernel, n_ca),
        out_shape=(
            jax.ShapeDtypeStruct((SQUARE, t, d), BF16),
            jax.ShapeDtypeStruct((n_ca,) + w.shape, BF16),
            jax.ShapeDtypeStruct((n_ca,) + off.shape, F32),
        ),
        in_specs=[any_spec, vmem, vmem],
        out_specs=(any_spec, vmem, vmem),
        scratch_shapes=[
            pltpu.VMEM((t, d), BF16),
            dma((3,)),
            dma((6,)),
            dma((6,)),
            dma((2, n_ca - 1)),
            dma((2, n_ca - 1)),
            dma((2, n_ca - 1)),
            dma((2, n_ca - 1)),
        ],
        compiler_params=pltpu.CompilerParams(
            collective_id=0, has_side_effects=True, vmem_limit_bytes=VMEM_LIMIT
        ),
        name="gather",
    )(images, w, off)


def features(x):
    wide = x.astype(F32)
    return jnp.concatenate([(wide * wide).astype(BF16), x], axis=1)


def score_kernel(x_ref, w_ref, off_ref, e_ref, peak_ref, lse_ref):
    feats = features(x_ref[...])
    s = lax.dot_general(w_ref[...], feats, (((1,), (1,)), ((), ())), preferred_element_type=F32)
    s = s + off_ref[...]
    peak = jnp.max(s, axis=0, keepdims=True)
    e = jnp.exp(s - peak)
    e_ref[...] = e
    peak_ref[...] = peak
    lse_ref[...] = peak + jnp.log(jnp.sum(e, axis=0, keepdims=True))


def score(x, w, off):
    rows, d = x.shape
    k = w.shape[0]
    n = min(CHUNK, rows)
    whole = lambda i: (0, 0)
    return pl.pallas_call(
        score_kernel,
        grid=(rows // n,),
        out_shape=(
            jax.ShapeDtypeStruct((k, rows), F32),
            jax.ShapeDtypeStruct((1, rows), F32),
            jax.ShapeDtypeStruct((1, rows), F32),
        ),
        in_specs=[
            pl.BlockSpec((n, d), lambda i: (i, 0)),
            pl.BlockSpec((k, 2 * d), whole),
            pl.BlockSpec((k, 1), whole),
        ],
        out_specs=(
            pl.BlockSpec((k, n), lambda i: (0, i)),
            pl.BlockSpec((1, n), lambda i: (0, i)),
            pl.BlockSpec((1, n), lambda i: (0, i)),
        ),
        compiler_params=pltpu.CompilerParams(vmem_limit_bytes=VMEM_LIMIT),
        name="score",
    )(x, w, off)


def lse_kernel(n_mp, lse_ref, peak_ref, logits_ref, factor_ref, like_ref, buf, send, recv):
    a, b, m = lax.axis_index("ca"), lax.axis_index("ib"), lax.axis_index("mp")
    n = SQUARE * n_mp
    me = b * n_mp + m

    def device(k):
        p = lax.rem(me + k, n)
        return (a, p // n_mp, lax.rem(p, n_mp))

    barrier = pltpu.get_barrier_semaphore()

    @pl.loop(1, n)
    def _(k):
        pl.semaphore_signal(barrier, inc=1, device_id=device(k), device_id_type=MESH)

    pl.semaphore_wait(barrier, n - 1)

    def copy(k):
        return remote(lse_ref, buf.at[k], send.at[k], recv.at[k], device(k))

    @pl.loop(1, n)
    def _(k):
        copy(k).start()

    logits = logits_ref[...]
    top = jnp.max(logits, axis=1, keepdims=True)
    logit_total = top + jnp.log(jnp.sum(jnp.exp(logits - top), axis=1, keepdims=True))

    @pl.loop(1, n)
    def _(k):
        copy(k).wait()

    own = lse_ref[...]
    high = lax.fori_loop(1, n, lambda k, h: jnp.maximum(h, buf[k]), own)
    total = lax.fori_loop(1, n, lambda k, t: t + jnp.exp(buf[k] - high), jnp.exp(own - high))
    row_total = high + jnp.log(total)
    factor_ref[...] = jnp.exp(peak_ref[...] - row_total)
    like_ref[...] = row_total - logit_total


def combine(lse, peak, logits, n_mp):
    n = SQUARE * n_mp
    vmem = pl.BlockSpec(memory_space=pltpu.VMEM)
    return pl.pallas_call(
        functools.partial(lse_kernel, n_mp),
        out_shape=(jax.ShapeDtypeStruct(lse.shape, F32),) * 2,
        in_specs=[vmem] * 3,
        out_specs=(vmem,) * 2,
        scratch_shapes=[
            pltpu.VMEM((n,) + lse.shape, F32),
            pltpu.SemaphoreType.DMA((n,)),
            pltpu.SemaphoreType.DMA((n,)),
        ],
        compiler_params=pltpu.CompilerParams(collective_id=1, has_side_effects=True),
        name="combine",
    )(lse, peak, logits[None, :])


def moment_kernel(x_ref, e_ref, factor_ref, mom_ref, cnt_ref, acc, cacc):
    i = pl.program_id(0)

    @pl.when(i == 0)
    def _():
        acc[...] = jnp.zeros_like(acc)
        cacc[...] = jnp.zeros_like(cacc)

    feats = features(x_ref[...])
    shares = (e_ref[...] * factor_ref[...]).astype(BF16)
    wide = shares.astype(F32)
    part = cacc[...]
    for j in range(wide.shape[1] // 128):
        part = part + wide[:, j * 128:(j + 1) * 128]
    cacc[...] = part
    acc[...] += jnp.dot(shares, feats, preferred_element_type=F32)

    @pl.when(i == pl.num_programs(0) - 1)
    def _():
        mom_ref[...] = acc[...].astype(BF16)
        cnt_ref[...] = jnp.sum(cacc[...], axis=1, keepdims=True)


def moment(x, e, factor):
    rows, d = x.shape
    k = e.shape[0]
    n = min(CHUNK, rows)
    return pl.pallas_call(
        moment_kernel,
        grid=(rows // n,),
        out_shape=(
            jax.ShapeDtypeStruct((k, 2 * d), BF16),
            jax.ShapeDtypeStruct((k, 1), F32),
        ),
        in_specs=[
            pl.BlockSpec((n, d), lambda i: (i, 0)),
            pl.BlockSpec((k, n), lambda i: (0, i)),
            pl.BlockSpec((1, n), lambda i: (0, i)),
        ],
        out_specs=(
            pl.BlockSpec((k, 2 * d), lambda i: (0, 0)),
            pl.BlockSpec((k, 1), lambda i: (0, 0)),
        ),
        scratch_shapes=[pltpu.VMEM((k, 2 * d), F32), pltpu.VMEM((k, 128), F32)],
        compiler_params=pltpu.CompilerParams(vmem_limit_bytes=VMEM_LIMIT),
        name="moment",
    )(x, e, factor)


def scatter_kernel(n_ca, mom_ref, cnt_ref, out_ref, cout_ref, loc, msend, mrecv, csend, crecv):
    a, b, m = lax.axis_index("ca"), lax.axis_index("ib"), lax.axis_index("mp")
    barrier = pltpu.get_barrier_semaphore()

    def other(k):
        return lax.rem(a + k, n_ca)

    @pl.loop(1, n_ca)
    def _(k):
        pl.semaphore_signal(barrier, inc=1, device_id=(other(k), b, m), device_id_type=MESH)

    own_m = pltpu.make_async_copy(mom_ref.at[a], out_ref.at[0], loc.at[0])
    own_c = pltpu.make_async_copy(cnt_ref.at[a], cout_ref.at[0], loc.at[1])
    own_m.start()
    own_c.start()
    pl.semaphore_wait(barrier, n_ca - 1)

    def copies(k):
        p = other(k)
        dev = (p, b, m)
        return (
            remote(cnt_ref.at[p], cout_ref.at[k], csend.at[k], crecv.at[k], dev),
            remote(mom_ref.at[p], out_ref.at[k], msend.at[k], mrecv.at[k], dev),
        )

    @pl.loop(1, n_ca)
    def _(k):
        for c in copies(k):
            c.start()

    @pl.loop(1, n_ca)
    def _(k):
        for c in copies(k):
            c.wait()

    own_m.wait()
    own_c.wait()


def scatter(mom, cnt, n_ca):
    vmem = pl.BlockSpec(memory_space=pltpu.VMEM)
    dma = pltpu.SemaphoreType.DMA
    return pl.pallas_call(
        functools.partial(scatter_kernel, n_ca),
        out_shape=(jax.ShapeDtypeStruct(mom.shape, BF16), jax.ShapeDtypeStruct(cnt.shape, F32)),
        in_specs=[vmem] * 2,
        out_specs=(vmem,) * 2,
        scratch_shapes=[dma((2,)), dma((n_ca,)), dma((n_ca,)), dma((n_ca,)), dma((n_ca,))],
        compiler_params=pltpu.CompilerParams(
            collective_id=2, has_side_effects=True, vmem_limit_bytes=VMEM_LIMIT
        ),
        name="scatter",
    )(mom, cnt)


def body(n_ca, n_mp, images, means, precisions, logits):
    t, d = images.shape
    r = means.shape[0]
    a, b, m = lax.axis_index("ca"), lax.axis_index("ib"), lax.axis_index("mp")
    own_logits = lax.dynamic_slice_in_dim(logits, ((m * n_ca + a) * SQUARE + b) * r, r)
    prec_b = precisions.astype(BF16)
    w = jnp.concatenate([-0.5 * prec_b, (means * precisions).astype(BF16)], axis=1)
    off = (
        own_logits
        + 0.5 * jnp.sum(jnp.log(precisions) - means * means * precisions, axis=1)
        - 0.5 * d * math.log(2.0 * math.pi)
    )
    imgs, w_all, off_all = gather(images, w, off[None, :], n_ca)
    x = imgs.reshape(SQUARE * t, d)
    e, peak, lse = score(x, w_all.reshape(n_ca * r, 2 * d), off_all.reshape(n_ca * r, 1))
    factor, like = combine(lse, peak, logits, n_mp)
    log_likelihood = lax.dynamic_slice_in_dim(like[0], b * t, t)
    mom, cnt = moment(x, e, factor)
    mom, cnt = scatter(mom.reshape(n_ca, r, 2 * d), cnt.reshape(n_ca, 1, r), n_ca)
    own_moments = jnp.sum(mom.astype(F32), axis=0)
    denominator = jnp.sum(cnt, axis=0)[0] + 1.0
    new_means = (own_moments[:, d:] + means) / denominator[:, None]
    second = (own_moments[:, :d] + 1.0 / precisions + means * means) / denominator[:, None]
    new_variances = second - new_means * new_means
    total = t * n_ca * SQUARE + logits.shape[0]
    new_log_weights = jnp.log(denominator) - jnp.log(jnp.float32(total))
    return (new_means, new_variances, new_log_weights, log_likelihood)


def solution(mesh):
    n_dp, n_mp = mesh.shape["dp"], mesh.shape["mp"]
    n_ca = n_dp // SQUARE
    split = Mesh(mesh.devices.reshape(n_ca, SQUARE, n_mp), ("ca", "ib", "mp"))
    dp = ("ca", "ib")
    comp = ("mp", "ca", "ib")
    return jax.shard_map(
        functools.partial(body, n_ca, n_mp),
        mesh=split,
        in_specs=(P(dp, None), P(comp, None), P(comp, None), P()),
        out_specs=(P(comp, None), P(comp, None), P(comp), P(dp)),
        check_vma=False,
    )
```

time: 429 us -> 151 us (0.35)
  the two profiles are of different devices: /device:TPU:0 before, /device:TPU:11 now
where the time goes in v1:
time: 151 us; the launch traced here: 150 us
  Pallas kernels  137 us (91%)
  other arithmetic  9.67 us (6%)
  local copies, waits for them, and re-layouts  3.03 us (2%)
    pallas_call x1, Pallas kernels, scatter(): pl.pallas_call(functools.partial(scatter_kernel, n_ca), out_shape=(jax.Sh...  40.1 us
    pallas_call x1, Pallas kernels, gather(): pl.pallas_call(functools.partial(gather_kernel, n_ca), out_shape=(jax.Sha...  36.8 us
    pallas_call x1, Pallas kernels, score(): pl.pallas_call(score_kernel, grid=(rows // n,), out_shape=(jax.ShapeDtype...  26.7 us
    pallas_call x1, Pallas kernels, moment(): pl.pallas_call(moment_kernel, grid=(rows // n,), out_shape=(jax.ShapeDtyp...  25.3 us
    pallas_call x1, Pallas kernels, combine(): pl.pallas_call(functools.partial(lse_kernel, n_mp), out_shape=(jax.ShapeD...  7.89 us

profile of v1, /device:TPU:11, one launch (start us, length us, event | category | flops | bytes accessed | tf_op | source)
XLA Modules:
  0.0 150.2 jit_solution(14919062984370563274)
XLA Ops:
  0.6 1.0 convert_multiply_fusion
  1.7 1.3 subtract_reduce_fusion
  3.0 1.3 add_add_fusion
  4.3 0.8 pad_maximum_fusion.w_ref
  5.1 36.8 %gather.1 = (bf16[4,2048,384]{2,1,0:T(8,128)(2,1)}, bf16[4,256,768]{2,1,0:T(8,128)(2,1)}, f32[4,1,256]{2,1,0:T(1,128)}) custom-call(bf16[2048,384]{1,0:T(8,128)(2,1)} %img_ref.1, bf16[256,768]{1,0:T(8,128)(2,1)} %pad_maximum_fusion.w_ref, f32[1,256]{1,0:T(1,128)} %bitcast.15), custom_call_target="tpu_custom_call" | custom-call | tf_op jit(solution)/shard_map/gather/pallas_call | solution.py:166
  41.9 1.7 %copy.8.off_ref = f32[1024,1]{1,0:T(8,128)} copy(f32[1024,1]{0,1:T(1,128)} %bitcast.16) | data formatting | bytes 8192 | tf_op jit(solution)/shard_map/reshape | solution.py:412
  43.6 26.7 %score.1 = (f32[1024,8192]{1,0:T(8,128)}, f32[1,8192]{1,0:T(1,128)}, f32[1,8192]{1,0:T(1,128)}) custom-call(bf16[8192,384]{1,0:T(8,128)(2,1)} %bitcast.8, bf16[1024,768]{1,0:T(8,128)(2,1)} %bitcast.10, f32[1024,1]{1,0:T(8,128)} %copy.8.off_ref), custom_call_target="tpu_custom_call" | custom-call | tf_op jit(solution)/shard_map/score/pallas_call | solution.py:213
  70.3 7.9 %combine.1 = (f32[1,8192]{1,0:T(1,128)}, f32[1,8192]{1,0:T(1,128)}) custom-call(f32[1,8192]{1,0:T(1,128)} %get-tuple-element.20.lse_ref, f32[1,8192]{1,0:T(1,128)} %get-tuple-element.21.peak_ref, f32[1,8192]{1,0:T(1,128)} %bitcast.12), custom_call_target="tpu_custom_call" | custom-call | tf_op jit(solution)/shard_map/combine/pallas_call | solution.py:279
  78.2 25.3 %moment.1 = (bf16[1024,768]{1,0:T(8,128)(2,1)}, f32[1024,1]{1,0:T(8,128)}) custom-call(bf16[8192,384]{1,0:T(8,128)(2,1)} %bitcast.9, f32[1024,8192]{1,0:T(8,128)} %get-tuple-element.19.e_ref, f32[1,8192]{1,0:T(1,128)} %get-tuple-element.22.factor_ref), custom_call_target="tpu_custom_call" | custom-call | tf_op jit(solution)/shard_map/moment/pallas_call | solution.py:321
  103.4 1.8 %reduce.1 = f32[1024]{0:T(1024)} reduce(f32[1024,1]{1,0:T(8,128)} %get-tuple-element.24, f32[]{:T(128)} %constant.37), dimensions={1}, to_apply=%get-tuple-element.24.reduce_sub_computation | reduce | bytes 8196 | tf_op jit(solution)/shard_map/moment/pallas_call | solution.py:321
  105.3 40.1 %scatter.1 = (bf16[4,256,768]{2,1,0:T(8,128)(2,1)}, f32[4,1,256]{2,1,0:T(1,128)}) custom-call(bf16[4,256,768]{2,1,0:T(8,128)(2,1)} %bitcast.11, f32[4,1,256]{2,1,0:T(1,128)} %bitcast.13), custom_call_target="tpu_custom_call" | custom-call | tf_op jit(solution)/shard_map/scatter/pallas_call | solution.py:385
  145.4 0.0 copy-start.2
  145.4 0.0 copy-start
  145.4 0.0 copy-start.1
  145.4 1.8 %convert_reduce_fusion = f32[256,768]{1,0:T(8,128)S(1)} fusion(bf16[4,256,768]{2,1,0:T(8,128)(2,1)} %get-tuple-element.25), kind=kLoop, calls=%fused_computation | loop fusion | flops 1376256 | bytes 2359296 | tf_op jit(solution)/shard_map/reduce_sum | solution.py:417
  147.2 0.0 copy-done.2
  147.2 0.6 log_add_fusion
  147.8 0.0 copy-done
  147.8 0.0 copy-done.1
  147.8 1.0 fusion.2
  148.9 1.3 constant_dynamic-slice_fusion
  (1 shorter events, 0.0 us)
Async XLA Ops:
  145.4 1.8 %copy-start.2 = (f32[4,1,256]{2,1,0:T(1,128)S(1)}, f32[4,1,256]{2,1,0:T(1,128)}, u32[]{:S(2)}) copy-start(f32[4,1,256]{2,1,0:T(1,128)} %get-tuple-element.26) | copy-start | bytes 12292
  145.4 2.4 %copy-start = (f32[256,384]{1,0:T(8,128)S(1)}, f32[256,384]{1,0:T(8,128)}, u32[]{:S(2)}) copy-start(f32[256,384]{1,0:T(8,128)} %param.6) | copy-start | bytes 1179652
  145.4 2.4 %copy-start.1 = (f32[256,384]{1,0:T(8,128)S(1)}, f32[256,384]{1,0:T(8,128)}, u32[]{:S(2)}) copy-start(f32[256,384]{1,0:T(8,128)} %param.5) | copy-start | bytes 1179652

commit v2 on v1

--- a/solution.py
+++ b/solution.py
@@ -291,108 +291,196 @@
     )(lse, peak, logits[None, :])
 
 
-def moment_kernel(x_ref, e_ref, factor_ref, mom_ref, cnt_ref, acc, cacc):
-    i = pl.program_id(0)
-
-    @pl.when(i == 0)
-    def _():
-        acc[...] = jnp.zeros_like(acc)
-        cacc[...] = jnp.zeros_like(cacc)
+def target(k, a, n):
+    left, right = a, n - 1 - a
+    far, near = jnp.maximum(left, right), jnp.minimum(left, right)
+    lead = far - near
+    late = jnp.maximum(k - lead, 0)
+    dist = jnp.where(k < lead, far - k, near - late // 2)
+    to_far = jnp.logical_or(k < lead, lax.rem(late, 2) == 0)
+    to_right = jnp.where(right >= left, to_far, jnp.logical_not(to_far))
+    return jnp.where(to_right, a + dist, a - dist)
+
+
+def moment_kernel(n_ca, total, x_ref, e_ref, factor_ref, means_ref, prec_ref,
+                  nm_ref, nv_ref, nw_ref, acc, cacc, crow, sbuf, sc, rbuf, rc,
+                  msend, mrecv, csend, crecv):
+    a, b, m = lax.axis_index("ca"), lax.axis_index("ib"), lax.axis_index("mp")
+    k, i = pl.program_id(0), pl.program_id(1)
+    last = pl.num_programs(1) - 1
+    d = means_ref.shape[1]
+    barrier = pltpu.get_barrier_semaphore()
+
+    @pl.when(jnp.logical_and(k == 0, i == 0))
+    def _():
+        @pl.when(a > 0)
+        def _():
+            pl.semaphore_signal(barrier, inc=1, device_id=(a - 1, b, m), device_id_type=MESH)
+
+        @pl.when(a < n_ca - 1)
+        def _():
+            pl.semaphore_signal(barrier, inc=1, device_id=(a + 1, b, m), device_id_type=MESH)
+
+        ends = (a == 0).astype(jnp.int32) + (a == n_ca - 1).astype(jnp.int32)
+        pl.semaphore_wait(barrier, 2 - ends)
+
+    def copies(j, way):
+        nbr = jnp.clip(a + 1 - 2 * way, 0, n_ca - 1)
+        dev = (nbr, b, m)
+        return (
+            remote(sbuf.at[j], rbuf.at[way, j], msend.at[j], mrecv.at[way, j], dev),
+            remote(sc.at[j], rc.at[way, j], csend.at[j], crecv.at[way, j], dev),
+        )
+
+    def info(q):
+        j = target(q, a, n_ca)
+        way = (j < a).astype(jnp.int32)
+        joined = jnp.where(j < a, a < n_ca - 1, a > 0)
+        return j, way, joined
+
+    def start(q):
+        j, way, _ = info(q)
+        for c in copies(j, way):
+            c.start()
+
+    def merge(q):
+        j, way, _ = info(q)
+        for c in copies(j, way):
+            c.wait_recv()
+        sbuf[j] = (acc[q] + rbuf[way, j].astype(F32)).astype(BF16)
+        sc[j] = crow[q] + rc[way, j]
+
+    @pl.when(jnp.logical_and(i == 0, k >= 1))
+    def _():
+        @pl.when(jnp.logical_not(info(k - 1)[2]))
+        def _():
+            start(k - 1)
+
+        @pl.when(jnp.logical_and(k >= 2, info(jnp.maximum(k - 2, 0))[2]))
+        def _():
+            start(k - 2)
 
     feats = features(x_ref[...])
     shares = (e_ref[...] * factor_ref[...]).astype(BF16)
     wide = shares.astype(F32)
-    part = cacc[...]
-    for j in range(wide.shape[1] // 128):
-        part = part + wide[:, j * 128:(j + 1) * 128]
-    cacc[...] = part
-    acc[...] += jnp.dot(shares, feats, preferred_element_type=F32)
-
-    @pl.when(i == pl.num_programs(0) - 1)
-    def _():
-        mom_ref[...] = acc[...].astype(BF16)
-        cnt_ref[...] = jnp.sum(cacc[...], axis=1, keepdims=True)
-
-
-def moment(x, e, factor):
+    part = wide[:, :128]
+    for q in range(1, wide.shape[1] // 128):
+        part = part + wide[:, q * 128:(q + 1) * 128]
+    prod = jnp.dot(shares, feats, preferred_element_type=F32)
+
+    @pl.when(i == 0)
+    def _():
+        acc[k] = prod
+        cacc[...] = part
+
+    @pl.when(i > 0)
+    def _():
+        acc[k] += prod
+        cacc[...] += part
+
+    @pl.when(i == last)
+    def _():
+        crow[k] = jnp.sum(cacc[...].T, axis=0, keepdims=True)
+
+        @pl.when(jnp.logical_and(k < n_ca - 1, jnp.logical_not(info(k)[2])))
+        def _():
+            j = info(k)[0]
+            sbuf[j] = acc[k].astype(BF16)
+            sc[j] = crow[k]
+
+        @pl.when(jnp.logical_and(k >= 1, info(jnp.maximum(k - 1, 0))[2]))
+        def _():
+            merge(k - 1)
+
+        @pl.when(k == n_ca - 1)
+        def _():
+            means, prec = means_ref[...], prec_ref[...]
+            nm_ref[...] = acc[n_ca - 1, :, d:] + means
+            nv_ref[...] = acc[n_ca - 1, :, :d] + 1.0 / prec + means * means
+
+            @pl.when(info(n_ca - 2)[2])
+            def _():
+                start(n_ca - 2)
+
+            def join(way):
+                for c in copies(a, way):
+                    c.wait_recv()
+                nm_ref[...] += rbuf[way, a, :, d:].astype(F32)
+                nv_ref[...] += rbuf[way, a, :, :d].astype(F32)
+                crow[n_ca - 1] += rc[way, a]
+
+            @pl.when(a > 0)
+            def _():
+                join(0)
+
+            @pl.when(a < n_ca - 1)
+            def _():
+                join(1)
+
+            denominator = crow[n_ca - 1] + 1.0
+            nw_ref[...] = jnp.log(denominator) - jnp.log(jnp.full_like(denominator, total))
+            rows = denominator.shape[1]
+            column = jnp.broadcast_to(denominator, (128, rows)).T
+            wide_column = jnp.concatenate([column] * (d // 128), axis=1)
+            new_means = nm_ref[...] / wide_column
+            nm_ref[...] = new_means
+            nv_ref[...] = nv_ref[...] / wide_column - new_means * new_means
+
+            @pl.loop(0, n_ca - 1)
+            def _(q):
+                j, way, _ = info(q)
+                for c in copies(j, way):
+                    c.wait_send()
+
+
+def moment(x, e, factor, means, precisions, n_ca, total):
     rows, d = x.shape
-    k = e.shape[0]
-    n = min(CHUNK, rows)
+    r = means.shape[0]
+    n = min(2048, rows)
+    dma = pltpu.SemaphoreType.DMA
+    fixed = lambda k, i: (0, 0)
+
+    def e_map(k, i):
+        return target(k, lax.axis_index("ca"), n_ca), i
+
     return pl.pallas_call(
-        moment_kernel,
-        grid=(rows // n,),
+        functools.partial(moment_kernel, n_ca, total),
+        grid=(n_ca, rows // n),
         out_shape=(
-            jax.ShapeDtypeStruct((k, 2 * d), BF16),
-            jax.ShapeDtypeStruct((k, 1), F32),
+            jax.ShapeDtypeStruct((r, d), F32),
+            jax.ShapeDtypeStruct((r, d), F32),
+            jax.ShapeDtypeStruct((1, r), F32),
         ),
         in_specs=[
-            pl.BlockSpec((n, d), lambda i: (i, 0)),
-            pl.BlockSpec((k, n), lambda i: (0, i)),
-            pl.BlockSpec((1, n), lambda i: (0, i)),
+            pl.BlockSpec((n, d), lambda k, i: (i, 0)),
+            pl.BlockSpec((r, n), e_map),
+            pl.BlockSpec((1, n), lambda k, i: (0, i)),
+            pl.BlockSpec((r, d), fixed),
+            pl.BlockSpec((r, d), fixed),
         ],
         out_specs=(
-            pl.BlockSpec((k, 2 * d), lambda i: (0, 0)),
-            pl.BlockSpec((k, 1), lambda i: (0, 0)),
-        ),
-        scratch_shapes=[pltpu.VMEM((k, 2 * d), F32), pltpu.VMEM((k, 128), F32)],
-        compiler_params=pltpu.CompilerParams(vmem_limit_bytes=VMEM_LIMIT),
-        name="moment",
-    )(x, e, factor)
-
-
-def scatter_kernel(n_ca, mom_ref, cnt_ref, out_ref, cout_ref, loc, msend, mrecv, csend, crecv):
-    a, b, m = lax.axis_index("ca"), lax.axis_index("ib"), lax.axis_index("mp")
-    barrier = pltpu.get_barrier_semaphore()
-
-    def other(k):
-        return lax.rem(a + k, n_ca)
-
-    @pl.loop(1, n_ca)
-    def _(k):
-        pl.semaphore_signal(barrier, inc=1, device_id=(other(k), b, m), device_id_type=MESH)
-
-    own_m = pltpu.make_async_copy(mom_ref.at[a], out_ref.at[0], loc.at[0])
-    own_c = pltpu.make_async_copy(cnt_ref.at[a], cout_ref.at[0], loc.at[1])
-    own_m.start()
-    own_c.start()
-    pl.semaphore_wait(barrier, n_ca - 1)
-
-    def copies(k):
-        p = other(k)
-        dev = (p, b, m)
-        return (
-            remote(cnt_ref.at[p], cout_ref.at[k], csend.at[k], crecv.at[k], dev),
-            remote(mom_ref.at[p], out_ref.at[k], msend.at[k], mrecv.at[k], dev),
-        )
-
-    @pl.loop(1, n_ca)
-    def _(k):
-        for c in copies(k):
-            c.start()
-
-    @pl.loop(1, n_ca)
-    def _(k):
-        for c in copies(k):
-            c.wait()
-
-    own_m.wait()
-    own_c.wait()
-
-
-def scatter(mom, cnt, n_ca):
-    vmem = pl.BlockSpec(memory_space=pltpu.VMEM)
-    dma = pltpu.SemaphoreType.DMA
-    return pl.pallas_call(
-        functools.partial(scatter_kernel, n_ca),
-        out_shape=(jax.ShapeDtypeStruct(mom.shape, BF16), jax.ShapeDtypeStruct(cnt.shape, F32)),
-        in_specs=[vmem] * 2,
-        out_specs=(vmem,) * 2,
-        scratch_shapes=[dma((2,)), dma((n_ca,)), dma((n_ca,)), dma((n_ca,)), dma((n_ca,))],
+            pl.BlockSpec((r, d), fixed),
+            pl.BlockSpec((r, d), fixed),
+            pl.BlockSpec((1, r), fixed),
+        ),
+        scratch_shapes=[
+            pltpu.VMEM((n_ca, r, 2 * d), F32),
+            pltpu.VMEM((r, 128), F32),
+            pltpu.VMEM((n_ca, 1, r), F32),
+            pltpu.VMEM((n_ca, r, 2 * d), BF16),
+            pltpu.VMEM((n_ca, 1, r), F32),
+            pltpu.VMEM((2, n_ca, r, 2 * d), BF16),
+            pltpu.VMEM((2, n_ca, 1, r), F32),
+            dma((n_ca,)),
+            dma((2, n_ca)),
+            dma((n_ca,)),
+            dma((2, n_ca)),
+        ],
         compiler_params=pltpu.CompilerParams(
             collective_id=2, has_side_effects=True, vmem_limit_bytes=VMEM_LIMIT
         ),
-        name="scatter",
-    )(mom, cnt)
+        name="moment",
+    )(x, e, factor, means, precisions)
 
 
 def body(n_ca, n_mp, images, means, precisions, logits):
@@ -412,16 +500,9 @@
     e, peak, lse = score(x, w_all.reshape(n_ca * r, 2 * d), off_all.reshape(n_ca * r, 1))
     factor, like = combine(lse, peak, logits, n_mp)
     log_likelihood = lax.dynamic_slice_in_dim(like[0], b * t, t)
-    mom, cnt = moment(x, e, factor)
-    mom, cnt = scatter(mom.reshape(n_ca, r, 2 * d), cnt.reshape(n_ca, 1, r), n_ca)
-    own_moments = jnp.sum(mom.astype(F32), axis=0)
-    denominator = jnp.sum(cnt, axis=0)[0] + 1.0
-    new_means = (own_moments[:, d:] + means) / denominator[:, None]
-    second = (own_moments[:, :d] + 1.0 / precisions + means * means) / denominator[:, None]
-    new_variances = second - new_means * new_means
-    total = t * n_ca * SQUARE + logits.shape[0]
-    new_log_weights = jnp.log(denominator) - jnp.log(jnp.float32(total))
-    return (new_means, new_variances, new_log_weights, log_likelihood)
+    total = float(t * n_ca * SQUARE + logits.shape[0])
+    new_means, new_variances, weights = moment(x, e, factor, means, precisions, n_ca, total)
+    return (new_means, new_variances, weights[0], log_likelihood)
 
 
 def solution(mesh):

time: 151 us -> 133 us (0.88)
  the two profiles are of different devices: /device:TPU:11 before, /device:TPU:0 now
where the time goes in v2:
time: 133 us
  Pallas kernels  120 us (90%)
  local copies, waits for them, and re-layouts  7.75 us (6%)
  other arithmetic  4.43 us (3%)
    pallas_call x1, Pallas kernels, moment(): pl.pallas_call(functools.partial(moment_kernel, n_ca, total), grid=(n_ca,...  47.4 us
    pallas_call x1, Pallas kernels, gather(): pl.pallas_call(functools.partial(gather_kernel, n_ca), out_shape=(jax.Sha...  38.7 us
    pallas_call x1, Pallas kernels, score(): pl.pallas_call(score_kernel, grid=(rows // n,), out_shape=(jax.ShapeDtype...  26.7 us
    pallas_call x1, Pallas kernels, combine(): pl.pallas_call(functools.partial(lse_kernel, n_mp), out_shape=(jax.ShapeD...  7.27 us
    unnamed x3, local copies, waits for them, and re-layouts  4.76 us

profile of v2, /device:TPU:0, one launch (start us, length us, event | category | flops | bytes accessed | tf_op | source)
XLA Modules:
  0.0 132.8 jit_solution(4559608700517301115)
XLA Ops:
  0.6 1.0 convert_multiply_fusion
  1.7 1.3 subtract_reduce_fusion
  3.0 1.3 %add_add_fusion = f32[256]{0:T(256)} fusion(f32[256]{0:T(256)S(1)} %get-tuple-element.26, f32[8192]{0:T(1024)} %param.7, s32[]{:T(128)S(6)} %select_n.6), kind=kLoop, calls=%fused_computation.4 | loop fusion | flops 768 | bytes 3076 | tf_op jit(solution)/shard_map/sub | solution.py:494
  4.3 0.8 pad_maximum_fusion.w_ref
  5.1 38.7 %gather.1 = (bf16[4,2048,384]{2,1,0:T(8,128)(2,1)}, bf16[4,256,768]{2,1,0:T(8,128)(2,1)}, f32[4,1,256]{2,1,0:T(1,128)}) custom-call(bf16[2048,384]{1,0:T(8,128)(2,1)} %img_ref.1, bf16[256,768]{1,0:T(8,128)(2,1)} %pad_maximum_fusion.w_ref, f32[1,256]{1,0:T(1,128)} %bitcast.12), custom_call_target="tpu_custom_call" | custom-call | tf_op jit(solution)/shard_map/gather/pallas_call | solution.py:166
  43.8 1.7 %copy.8.off_ref = f32[1024,1]{1,0:T(8,128)} copy(f32[1024,1]{0,1:T(1,128)} %bitcast.13) | data formatting | bytes 8192 | tf_op jit(solution)/shard_map/reshape | solution.py:500
  45.5 26.7 %score.1 = (f32[1024,8192]{1,0:T(8,128)}, f32[1,8192]{1,0:T(1,128)}, f32[1,8192]{1,0:T(1,128)}) custom-call(bf16[8192,384]{1,0:T(8,128)(2,1)} %bitcast.7, bf16[1024,768]{1,0:T(8,128)(2,1)} %bitcast.9, f32[1024,1]{1,0:T(8,128)} %copy.8.off_ref), custom_call_target="tpu_custom_call" | custom-call | tf_op jit(solution)/shard_map/score/pallas_call | solution.py:213
  72.1 7.3 %combine.1 = (f32[1,8192]{1,0:T(1,128)}, f32[1,8192]{1,0:T(1,128)}) custom-call(f32[1,8192]{1,0:T(1,128)} %get-tuple-element.19.lse_ref, f32[1,8192]{1,0:T(1,128)} %get-tuple-element.20.peak_ref, f32[1,8192]{1,0:T(1,128)} %bitcast.10), custom_call_target="tpu_custom_call" | custom-call | tf_op jit(solution)/shard_map/combine/pallas_call | solution.py:279
  79.4 47.4 %moment.1 = (f32[256,384]{1,0:T(8,128)}, f32[256,384]{1,0:T(8,128)}, f32[1,256]{1,0:T(1,128)}) custom-call(bf16[8192,384]{1,0:T(8,128)(2,1)} %bitcast.8, f32[1024,8192]{1,0:T(8,128)} %get-tuple-element.18.e_ref, f32[1,8192]{1,0:T(1,128)} %get-tuple-element.21.factor_ref, f32[256,384]{1,0:T(8,128)} %means_ref.1, f32[256,384]{1,0:T(8,128)} %prec_ref.1), custom_call_target="tpu_custom_call" | custom-call | tf_op jit(solution)/shard_map/moment/pallas_call | solution.py:446
  126.8 1.3 constant_dynamic-slice_fusion
  128.1 1.8 %copy.12 = f32[256,384]{1,0:T(8,128)} copy(f32[256,384]{1,0:T(8,128)} %get-tuple-element.32) | data formatting | bytes 786432
  129.8 1.8 %copy.13 = f32[256,384]{1,0:T(8,128)} copy(f32[256,384]{1,0:T(8,128)} %get-tuple-element.33) | data formatting | bytes 786432
  131.6 1.2 copy.14

commit v3 on v2

--- a/solution.py
+++ b/solution.py
@@ -10,7 +10,7 @@
 
 MESH = pl.DeviceIdType.MESH
 SQUARE = 4
-CHUNK = 512
+PIECES = 2
 F32 = jnp.float32
 BF16 = jnp.bfloat16
 VMEM_LIMIT = 60 * 1024 * 1024
@@ -22,17 +22,35 @@
     )
 
 
-def gather_kernel(n_ca, img_ref, w_ref, off_ref, imgs_ref, wall_ref, offall_ref, stage,
-                  loc, isend, irecv, wsend, wrecv, osend, orecv):
+def features(x):
+    wide = x.astype(F32)
+    return jnp.concatenate([(wide * wide).astype(BF16), x], axis=1)
+
+
+def target(k, a, n):
+    left, right = a, n - 1 - a
+    far, near = jnp.maximum(left, right), jnp.minimum(left, right)
+    lead = far - near
+    late = jnp.maximum(k - lead, 0)
+    dist = jnp.where(k < lead, far - k, near - late // 2)
+    to_far = jnp.logical_or(k < lead, lax.rem(late, 2) == 0)
+    to_right = jnp.where(right >= left, to_far, jnp.logical_not(to_far))
+    return jnp.where(to_right, a + dist, a - dist)
+
+
+def score_kernel(n_ca, img_ref, w_ref, off_ref, imgs_out, e_out, peak_ref, lse_ref,
+                 imgs, wall, offall, ebuf, blk_lse, loc, isend, irecv,
+                 wsend, wrecv, osend, orecv, esem, psem):
     a, b, m = lax.axis_index("ca"), lax.axis_index("ib"), lax.axis_index("mp")
+    t_rows = img_ref.shape[0]
+    r = w_ref.shape[0]
     core = lax.rem(m, 2)
     partner = m + 1 - 2 * core
     bx = b + 1 - 2 * lax.rem(b, 2)
     by = lax.rem(b + 2, 4)
     bd = lax.rem(bx + 2, 4)
     to_x, to_y, to_p = (a, bx, m), (a, by, m), (a, b, partner)
-    half_rows = img_ref.shape[0] // 2
-    half = pl.ds(pl.multiple_of(core * half_rows, half_rows), half_rows)
+    sub = t_rows // (2 * PIECES)
 
     barrier = pltpu.get_barrier_semaphore()
     for dev in (to_x, to_y, to_p):
@@ -46,191 +64,220 @@
     def _():
         pl.semaphore_signal(barrier, inc=1, device_id=(a + 1, b, m), device_id_type=MESH)
 
-    own_in = pltpu.make_async_copy(img_ref, stage, loc.at[0])
-    own_in.start()
-    own_w = pltpu.make_async_copy(w_ref, wall_ref.at[a], loc.at[1])
-    own_w.start()
-    own_o = pltpu.make_async_copy(off_ref, offall_ref.at[a], loc.at[2])
-    own_o.start()
-
+    own = (
+        pltpu.make_async_copy(img_ref, imgs.at[b], loc.at[0]),
+        pltpu.make_async_copy(w_ref, wall.at[a], loc.at[1]),
+        pltpu.make_async_copy(off_ref, offall.at[a], loc.at[2]),
+    )
+    for c in own:
+        c.start()
     ends = (a == 0).astype(jnp.int32) + (a == n_ca - 1).astype(jnp.int32)
     pl.semaphore_wait(barrier, 5 - ends)
 
-    def shard(i, src_own=False):
-        src = img_ref.at[half] if src_own else imgs_ref.at[i, half]
-        return src, imgs_ref.at[i, half]
-
-    def img_copy(k, i, dev, src_own=False):
-        src, dst = shard(i, src_own)
-        return remote(src, dst, isend.at[k], irecv.at[k], dev)
-
-    send_x = img_copy(0, b, to_x, True)
-    send_y = img_copy(1, b, to_y, True)
-    send_x.start()
-    send_y.start()
-
-    def chain(direction, s):
-        blk = a - s if direction == 0 else a + s
-        blk_ok = (blk >= 0) if direction == 0 else (blk < n_ca)
-        nbr_ok = (a < n_ca - 1) if direction == 0 else (a > 0)
-        nbr = a + 1 if direction == 0 else a - 1
-        blk_c = jnp.clip(blk, 0, n_ca - 1)
-        src_w = w_ref if s == 0 else wall_ref.at[blk_c]
-        src_o = off_ref if s == 0 else offall_ref.at[blk_c]
-        dev = (nbr, b, m)
-        cw = remote(src_w, wall_ref.at[blk_c], wsend.at[direction, s], wrecv.at[direction, s], dev)
-        co = remote(src_o, offall_ref.at[blk_c], osend.at[direction, s], orecv.at[direction, s], dev)
-        return jnp.logical_and(blk_ok, nbr_ok), cw, co
-
-    def chain_recv(direction, s):
-        blk = a - 1 - s if direction == 0 else a + 1 + s
-        ok = (blk >= 0) if direction == 0 else (blk < n_ca)
-        blk_c = jnp.clip(blk, 0, n_ca - 1)
-        nbr = jnp.clip(a + 1 if direction == 0 else a - 1, 0, n_ca - 1)
-        dev = (nbr, b, m)
-        cw = remote(w_ref, wall_ref.at[blk_c], wsend.at[direction, s], wrecv.at[direction, s], dev)
-        co = remote(off_ref, offall_ref.at[blk_c], osend.at[direction, s], orecv.at[direction, s], dev)
-        return ok, cw, co
-
-    def start_chain(s):
-        for d in (0, 1):
-            ok, cw, co = chain(d, s)
+    def img_copy(k, i, dev, piece, first=False):
+        rows = pl.ds(pl.multiple_of((core * PIECES + piece) * sub, sub), sub)
+        dst = imgs.at[i, rows]
+        return remote(img_ref.at[rows] if first else dst, dst, isend.at[k, piece], irecv.at[k, piece], dev)
+
+    def chain(way, s, blk, first=False):
+        blk = jnp.clip(blk, 0, n_ca - 1)
+        dev = (jnp.clip(a + 1 - 2 * way, 0, n_ca - 1), b, m)
+        return (
+            remote(w_ref if first else wall.at[blk], wall.at[blk], wsend.at[way, s], wrecv.at[way, s], dev),
+            remote(off_ref if first else offall.at[blk], offall.at[blk], osend.at[way, s], orecv.at[way, s], dev),
+        )
+
+    def has_next(way):
+        return jnp.where(way == 0, a < n_ca - 1, a > 0)
+
+    for way in (0, 1):
+        @pl.when(has_next(way))
+        def _():
+            for c in chain(way, 0, a, True):
+                c.start()
+
+    for piece in range(PIECES):
+        img_copy(0, b, to_x, piece, True).start()
+        img_copy(1, b, to_y, piece, True).start()
+    for c in own:
+        c.wait()
+
+    def place(q):
+        j = target(n_ca - 1 - q, a, n_ca)
+        return j, (j > a).astype(jnp.int32)
+
+    def take(q):
+        j, way = place(q)
+        s = jnp.maximum(jnp.abs(a - j) - 1, 0)
+        for c in chain(way, s, j):
+            c.wait_recv()
+
+        @pl.when(has_next(way))
+        def _():
+            for c in chain(way, s + 1, j):
+                c.start()
+
+    def images_in(piece):
+        img_copy(0, bx, to_x, piece).wait_recv()
+        img_copy(3, bx, to_p, piece).start()
+
+        @pl.when(core == 0)
+        def _():
+            img_copy(2, bx, to_y, piece).start()
+
+        img_copy(1, by, to_y, piece).wait_recv()
+        img_copy(4, by, to_p, piece).start()
+
+        @pl.when(core == 1)
+        def _():
+            img_copy(2, by, to_x, piece).start()
+
+    def corner_in(piece):
+        img_copy(2, bd, to_x, piece).wait_recv()
+        img_copy(5, bd, to_p, piece).start()
+
+    def paired(k, i):
+        for piece in range(PIECES):
+            img_copy(k, i, to_p, piece).wait_recv()
+
+    def put(i, slot):
+        return pltpu.make_async_copy(imgs.at[i], imgs_out.at[i], psem.at[slot])
+
+    def shard(p):
+        return jnp.where(p == 0, b, jnp.where(p == 1, bx, jnp.where(p == 2, by, bd)))
+
+    near = n_ca - 1
+
+    def e_copy(t, j, i):
+        slot = lax.rem(t, 2)
+        rows = pl.ds(pl.multiple_of(j * r, r), r)
+        cols = pl.ds(pl.multiple_of(i * t_rows, t_rows), t_rows)
+        return pltpu.make_async_copy(ebuf.at[slot], e_out.at[rows, cols], esem.at[slot])
+
+    @pl.loop(0, 4 * n_ca)
+    def _(t):
+        p = jnp.where(t < 3 * near, t // near, jnp.where(t < 3 * n_ca, t - 3 * near, 3))
+        q = jnp.where(t < 3 * near, lax.rem(t, near), jnp.where(t < 3 * n_ca, near, t - 3 * n_ca))
+
+        @pl.when(t == near - 1)
+        def _():
+            for piece in range(PIECES - 1):
+                images_in(piece)
+
+        @pl.when(jnp.logical_and(t >= 1, t < near))
+        def _():
+            take(jnp.clip(t, 1, near))
+
+        @pl.when(t == near)
+        def _():
+            put(b, 0).start()
+            images_in(PIECES - 1)
+
+            @pl.when(has_next(place(near)[1]))
+            def _():
+                take(near)
+
+            paired(3, bx)
+
+        @pl.when(t == 2 * near)
+        def _():
+            put(bx, 1).start()
+            for piece in range(PIECES - 1):
+                corner_in(piece)
+            paired(4, by)
+
+        @pl.when(t == 3 * near)
+        def _():
+            put(by, 2).start()
+            corner_in(PIECES - 1)
+
+            @pl.when(jnp.logical_not(has_next(place(near)[1])))
+            def _():
+                take(near)
+
+        @pl.when(t == 3 * n_ca)
+        def _():
+            paired(5, bd)
+            put(bd, 3).start()
+
+        i = shard(p)
+        j = place(q)[0]
+
+        @pl.when(t >= 2)
+        def _():
+            e_copy(t, j, i).wait()
+
+        cols = pl.ds(pl.multiple_of(i * t_rows, t_rows), t_rows)
+        feats = features(imgs[i])
+        s = lax.dot_general(wall[j], feats, (((1,), (1,)), ((), ())), preferred_element_type=F32)
+        column = jnp.broadcast_to(offall[j], (128, r)).T
+        s = s + column[:, :1]
+        peak = jnp.max(s, axis=0, keepdims=True)
+        e = jnp.exp(s - peak)
+        ebuf[lax.rem(t, 2)] = e
+        peak_ref[j, :, cols] = peak
+        blk_lse[j, :, cols] = peak + jnp.log(jnp.sum(e, axis=0, keepdims=True))
+        e_copy(t, j, i).start()
+
+    high = lax.fori_loop(1, n_ca, lambda k, h: jnp.maximum(h, blk_lse[k]), blk_lse[0])
+    tot = lax.fori_loop(1, n_ca, lambda k, x: x + jnp.exp(blk_lse[k] - high), jnp.exp(blk_lse[0] - high))
+    lse_ref[...] = high + jnp.log(tot)
+
+    for t in (0, 1):
+        e_copy(t, a, b).wait()
+    for slot, i in enumerate((b, bx, by, bd)):
+        put(i, slot).wait()
+    for k, i in enumerate((b, b, bd, bx, by, bd)):
+        for piece in range(PIECES):
+            img_copy(k, i, to_p, piece).wait_send()
+    for way in (0, 1):
+        @pl.loop(0, n_ca - 1)
+        def _(s):
+            blk = a - s + 2 * way * s
+            ok = jnp.logical_and(has_next(way), jnp.logical_and(blk >= 0, blk < n_ca))
 
             @pl.when(ok)
             def _():
-                cw.start()
-                co.start()
-
-    def wait_chain(s):
-        for d in (0, 1):
-            ok, cw, co = chain_recv(d, s)
-
-            @pl.when(ok)
-            def _():
-                cw.wait_recv()
-                co.wait_recv()
-
-    start_chain(0)
-    own_in.wait()
-    own_out = pltpu.make_async_copy(stage, imgs_ref.at[b], loc.at[0])
-    own_out.start()
-    wait_chain(0)
-    if n_ca > 2:
-        start_chain(1)
-    send_x.wait_recv()
-    pass_x = img_copy(3, bx, to_p)
-    pass_x.start()
-
-    @pl.when(core == 0)
-    def _():
-        img_copy(2, bx, to_y).start()
-
-    send_y.wait_recv()
-    pass_y = img_copy(4, by, to_p)
-    pass_y.start()
-
-    @pl.when(core == 1)
-    def _():
-        img_copy(2, by, to_x).start()
-
-    for s in range(1, n_ca - 1):
-        wait_chain(s)
-        if s + 1 < n_ca - 1:
-            start_chain(s + 1)
-    relay = img_copy(2, bd, to_x)
-    relay.wait_recv()
-    pass_d = img_copy(5, bd, to_p)
-    pass_d.start()
-    for c in (pass_x, pass_y, pass_d):
-        c.wait()
-    for c in (send_x, send_y, relay):
-        c.wait_send()
-    for s in range(n_ca - 1):
-        for d in (0, 1):
-            ok, cw, co = chain(d, s)
-
-            @pl.when(ok)
-            def _():
-                cw.wait_send()
-                co.wait_send()
-    own_out.wait()
-    own_w.wait()
-    own_o.wait()
-
-
-def gather(images, w, off, n_ca):
+                for c in chain(way, s, blk):
+                    c.wait_send()
+
+
+def score(images, w, off, n_ca):
     t, d = images.shape
+    r = w.shape[0]
+    rows = SQUARE * t
     any_spec = pl.BlockSpec(memory_space=pl.ANY)
     vmem = pl.BlockSpec(memory_space=pltpu.VMEM)
     dma = pltpu.SemaphoreType.DMA
+    line = dma((2, n_ca - 1))
     return pl.pallas_call(
-        functools.partial(gather_kernel, n_ca),
+        functools.partial(score_kernel, n_ca),
         out_shape=(
             jax.ShapeDtypeStruct((SQUARE, t, d), BF16),
-            jax.ShapeDtypeStruct((n_ca,) + w.shape, BF16),
-            jax.ShapeDtypeStruct((n_ca,) + off.shape, F32),
+            jax.ShapeDtypeStruct((n_ca * r, rows), F32),
+            jax.ShapeDtypeStruct((n_ca, 1, rows), F32),
+            jax.ShapeDtypeStruct((1, rows), F32),
         ),
         in_specs=[any_spec, vmem, vmem],
-        out_specs=(any_spec, vmem, vmem),
+        out_specs=(any_spec, any_spec, vmem, vmem),
         scratch_shapes=[
-            pltpu.VMEM((t, d), BF16),
+            pltpu.VMEM((SQUARE, t, d), BF16),
+            pltpu.VMEM((n_ca, r, 2 * d), BF16),
+            pltpu.VMEM((n_ca, 1, r), F32),
+            pltpu.VMEM((2, r, t), F32),
+            pltpu.VMEM((n_ca, 1, rows), F32),
             dma((3,)),
-            dma((6,)),
-            dma((6,)),
-            dma((2, n_ca - 1)),
-            dma((2, n_ca - 1)),
-            dma((2, n_ca - 1)),
-            dma((2, n_ca - 1)),
+            dma((6, PIECES)),
+            dma((6, PIECES)),
+            line, line, line, line,
+            dma((2,)),
+            dma((4,)),
         ],
         compiler_params=pltpu.CompilerParams(
             collective_id=0, has_side_effects=True, vmem_limit_bytes=VMEM_LIMIT
         ),
-        name="gather",
+        name="score",
     )(images, w, off)
-
-
-def features(x):
-    wide = x.astype(F32)
-    return jnp.concatenate([(wide * wide).astype(BF16), x], axis=1)
-
-
-def score_kernel(x_ref, w_ref, off_ref, e_ref, peak_ref, lse_ref):
-    feats = features(x_ref[...])
-    s = lax.dot_general(w_ref[...], feats, (((1,), (1,)), ((), ())), preferred_element_type=F32)
-    s = s + off_ref[...]
-    peak = jnp.max(s, axis=0, keepdims=True)
-    e = jnp.exp(s - peak)
-    e_ref[...] = e
-    peak_ref[...] = peak
-    lse_ref[...] = peak + jnp.log(jnp.sum(e, axis=0, keepdims=True))
-
-
-def score(x, w, off):
-    rows, d = x.shape
-    k = w.shape[0]
-    n = min(CHUNK, rows)
-    whole = lambda i: (0, 0)
-    return pl.pallas_call(
-        score_kernel,
-        grid=(rows // n,),
-        out_shape=(
-            jax.ShapeDtypeStruct((k, rows), F32),
-            jax.ShapeDtypeStruct((1, rows), F32),
-            jax.ShapeDtypeStruct((1, rows), F32),
-        ),
-        in_specs=[
-            pl.BlockSpec((n, d), lambda i: (i, 0)),
-            pl.BlockSpec((k, 2 * d), whole),
-            pl.BlockSpec((k, 1), whole),
-        ],
-        out_specs=(
-            pl.BlockSpec((k, n), lambda i: (0, i)),
-            pl.BlockSpec((1, n), lambda i: (0, i)),
-            pl.BlockSpec((1, n), lambda i: (0, i)),
-        ),
-        compiler_params=pltpu.CompilerParams(vmem_limit_bytes=VMEM_LIMIT),
-        name="score",
-    )(x, w, off)
 
 
 def lse_kernel(n_mp, lse_ref, peak_ref, logits_ref, factor_ref, like_ref, buf, send, recv):
@@ -269,7 +316,7 @@
     high = lax.fori_loop(1, n, lambda k, h: jnp.maximum(h, buf[k]), own)
     total = lax.fori_loop(1, n, lambda k, t: t + jnp.exp(buf[k] - high), jnp.exp(own - high))
     row_total = high + jnp.log(total)
-    factor_ref[...] = jnp.exp(peak_ref[...] - row_total)
+    factor_ref[...] = jnp.exp(peak_ref[...] - row_total[None])
     like_ref[...] = row_total - logit_total
 
 
@@ -278,7 +325,7 @@
     vmem = pl.BlockSpec(memory_space=pltpu.VMEM)
     return pl.pallas_call(
         functools.partial(lse_kernel, n_mp),
-        out_shape=(jax.ShapeDtypeStruct(lse.shape, F32),) * 2,
+        out_shape=(jax.ShapeDtypeStruct(peak.shape, F32), jax.ShapeDtypeStruct(lse.shape, F32)),
         in_specs=[vmem] * 3,
         out_specs=(vmem,) * 2,
         scratch_shapes=[
@@ -291,17 +338,6 @@
     )(lse, peak, logits[None, :])
 
 
-def target(k, a, n):
-    left, right = a, n - 1 - a
-    far, near = jnp.maximum(left, right), jnp.minimum(left, right)
-    lead = far - near
-    late = jnp.maximum(k - lead, 0)
-    dist = jnp.where(k < lead, far - k, near - late // 2)
-    to_far = jnp.logical_or(k < lead, lax.rem(late, 2) == 0)
-    to_right = jnp.where(right >= left, to_far, jnp.logical_not(to_far))
-    return jnp.where(to_right, a + dist, a - dist)
-
-
 def moment_kernel(n_ca, total, x_ref, e_ref, factor_ref, means_ref, prec_ref,
                   nm_ref, nv_ref, nw_ref, acc, cacc, crow, sbuf, sc, rbuf, rc,
                   msend, mrecv, csend, crecv):
@@ -361,7 +397,7 @@
             start(k - 2)
 
     feats = features(x_ref[...])
-    shares = (e_ref[...] * factor_ref[...]).astype(BF16)
+    shares = (e_ref[...] * factor_ref[0]).astype(BF16)
     wide = shares.astype(F32)
     part = wide[:, :128]
     for q in range(1, wide.shape[1] // 128):
@@ -442,6 +478,9 @@
 
     def e_map(k, i):
         return target(k, lax.axis_index("ca"), n_ca), i
+
+    def f_map(k, i):
+        return target(k, lax.axis_index("ca"), n_ca), 0, i
 
     return pl.pallas_call(
         functools.partial(moment_kernel, n_ca, total),
@@ -454,7 +493,7 @@
         in_specs=[
             pl.BlockSpec((n, d), lambda k, i: (i, 0)),
             pl.BlockSpec((r, n), e_map),
-            pl.BlockSpec((1, n), lambda k, i: (0, i)),
+            pl.BlockSpec((1, 1, n), f_map),
             pl.BlockSpec((r, d), fixed),
             pl.BlockSpec((r, d), fixed),
         ],
@@ -495,9 +534,8 @@
         + 0.5 * jnp.sum(jnp.log(precisions) - means * means * precisions, axis=1)
         - 0.5 * d * math.log(2.0 * math.pi)
     )
-    imgs, w_all, off_all = gather(images, w, off[None, :], n_ca)
+    imgs, e, peak, lse = score(images, w, off[None, :], n_ca)
     x = imgs.reshape(SQUARE * t, d)
-    e, peak, lse = score(x, w_all.reshape(n_ca * r, 2 * d), off_all.reshape(n_ca * r, 1))
     factor, like = combine(lse, peak, logits, n_mp)
     log_likelihood = lax.dynamic_slice_in_dim(like[0], b * t, t)
     total = float(t * n_ca * SQUARE + logits.shape[0])

time: 133 us -> 116 us (0.87)
  Pallas kernels: 120 us -> 104 us
  local copies, waits for them, and re-layouts: 7.75 us -> 6.07 us
    pallas_call x2 -> x1, Pallas kernels: 65.3 us -> 48.4 us  [score(): pl.pallas_call(functools.partial(score_kernel, n_ca), out_shape=(jax.Shap...]
    pallas_call x1, Pallas kernels: 7.27 us -> 9.56 us  [combine(): pl.pallas_call(functools.partial(lse_kernel, n_mp), out_shape=(jax.ShapeD...]
    reshape x1 -> x0, local copies, waits for them, and re-layouts: 1.7 us -> none  [body(): off_all.reshape(n_ca * r, 1)]
where the time goes in v3:
time: 116 us; the launch traced here: 115 us
  Pallas kernels  104 us (90%)
  local copies, waits for them, and re-layouts  6.07 us (5%)
  other arithmetic  4.43 us (4%)
    pallas_call x1, Pallas kernels, score(): pl.pallas_call(functools.partial(score_kernel, n_ca), out_shape=(jax.Shap...  48.4 us
    pallas_call x1, Pallas kernels, moment(): pl.pallas_call(functools.partial(moment_kernel, n_ca, total), grid=(n_ca,...  46.3 us
    pallas_call x1, Pallas kernels, combine(): pl.pallas_call(functools.partial(lse_kernel, n_mp), out_shape=(jax.ShapeD...  9.56 us
    unnamed x3, local copies, waits for them, and re-layouts  4.76 us

profile of v3, /device:TPU:0, one launch (start us, length us, event | category | flops | bytes accessed | tf_op | source)
XLA Modules:
  0.0 115.5 jit_solution(1042490580716367053)
XLA Ops:
  0.6 1.0 convert_multiply_fusion
  1.7 1.3 %subtract_reduce_fusion = (f32[256]{0:T(256)S(1)}, bf16[256,384]{1,0:T(8,128)(2,1)S(1)}) fusion(f32[256,384]{1,0:T(8,128)} %prec_ref.1, f32[256,384]{1,0:T(8,128)} %means_ref.1), kind=kLoop, calls=%fused_computation.1 | loop fusion | flops 589568 | bytes 984064 | tf_op jit(solution)/shard_map/reduce_sum | solution.py:534
  3.0 1.3 %add_add_fusion = f32[256]{0:T(256)} fusion(f32[256]{0:T(256)S(1)} %get-tuple-element.22, f32[8192]{0:T(1024)} %param.7, s32[]{:T(128)S(6)} %select_n.6), kind=kLoop, calls=%fused_computation.4 | loop fusion | flops 768 | bytes 3076 | tf_op jit(solution)/shard_map/sub | solution.py:533
  4.3 0.8 pad_maximum_fusion.w_ref
  5.1 48.4 %score.1 = (bf16[4,2048,384]{2,1,0:T(8,128)(2,1)}, f32[1024,8192]{1,0:T(8,128)}, f32[4,1,8192]{2,1,0:T(1,128)}, f32[1,8192]{1,0:T(1,128)}) custom-call(bf16[2048,384]{1,0:T(8,128)(2,1)} %img_ref.1, bf16[256,768]{1,0:T(8,128)(2,1)} %pad_maximum_fusion.w_ref, f32[1,256]{1,0:T(1,128)} %bitcast.8), custom_call_target="tpu_custom_call" | custom-call | tf_op jit(solution)/shard_map/score/pallas_call | solution.py:253
  53.5 9.6 %combine.1 = (f32[4,1,8192]{2,1,0:T(1,128)}, f32[1,8192]{1,0:T(1,128)}) custom-call(f32[1,8192]{1,0:T(1,128)} %get-tuple-element.15.lse_ref, f32[4,1,8192]{2,1,0:T(1,128)} %get-tuple-element.16.peak_ref, f32[1,8192]{1,0:T(1,128)} %bitcast.6), custom_call_target="tpu_custom_call" | custom-call | tf_op jit(solution)/shard_map/combine/pallas_call | solution.py:326
  63.1 46.3 %moment.1 = (f32[256,384]{1,0:T(8,128)}, f32[256,384]{1,0:T(8,128)}, f32[1,256]{1,0:T(1,128)}) custom-call(bf16[8192,384]{1,0:T(8,128)(2,1)} %bitcast.5, f32[1024,8192]{1,0:T(8,128)} %get-tuple-element.14.e_ref, f32[4,1,8192]{2,1,0:T(1,128)} %get-tuple-element.17.factor_ref, f32[256,384]{1,0:T(8,128)} %means_ref.1, f32[256,384]{1,0:T(8,128)} %prec_ref.1), custom_call_target="tpu_custom_call" | custom-call | tf_op jit(solution)/shard_map/moment/pallas_call | solution.py:485
  109.4 1.3 %constant_dynamic-slice_fusion = f32[1,2048]{1,0:T(1,128)} fusion(f32[1,8192]{1,0:T(1,128)} %get-tuple-element.21, s32[]{:T(128)S(6)} %select_n.7), kind=kLoop, calls=%fused_computation.5 | loop fusion | bytes 16388 | tf_op jit(solution)/shard_map/dynamic_slice | solution.py:540
  110.7 1.8 %copy.11 = f32[256,384]{1,0:T(8,128)} copy(f32[256,384]{1,0:T(8,128)} %get-tuple-element.28) | data formatting | bytes 786432
  112.5 1.8 %copy.12 = f32[256,384]{1,0:T(8,128)} copy(f32[256,384]{1,0:T(8,128)} %get-tuple-element.29) | data formatting | bytes 786432
  114.3 1.2 %copy.13 = f32[256]{0:T(256)} copy(f32[256]{0:T(256)} %bitcast.9) | data formatting | bytes 2048
